TPU v7x, 512 devices: a whole 4x8x8 slice. The times are simulated.
512 devices in a mesh: lat: 16 (over y, x_hi), lon: 32 (over z, x_lo, core).
Axes of the slice: x: 4 (x_hi: 2, x_lo: 2; x = x_hi * 2 + x_lo), y: 8, z: 8, core: 2. Of those that a mesh axis runs over, the one named last changes fastest.
Arguments:
- tokens: bfloat16 [2, 192, 768, 512], P(None, 'lat', 'lon'), may hold values from -6 to 6
- level_ids: int32 [2, 192, 768], P(None, 'lat', 'lon'), may hold values from 0 to 2
- coarse_ids: int32 [2, 96, 384], P(None, 'lat', 'lon'), may hold values from 0 to 2
- first_qkv: bfloat16 [512, 1536], replicated, may hold values from -1.25 to 1.25
- first_out: bfloat16 [512, 512], replicated, may hold values from -0.25 to 0.25
- merge_weight: bfloat16 [2048, 1024], P('lon'), may hold values from -0.125 to 0.125
- second_qkv: bfloat16 [1024, 3072], P('lon'), may hold values from -1.25 to 1.25
- second_out: bfloat16 [1024, 1024], P('lon'), may hold values from -0.1875 to 0.1875
Outputs:
- skip: bfloat16 [2, 192, 768, 512], P(None, 'lat', 'lon')
- coarse: bfloat16 [2, 96, 384, 1024], P(None, 'lat', 'lon')
All inputs are finite; a program needn't handle non-finite values.
Results may differ from a plain program's by a relative error of at most 0.012.
Values may be sent and summed in bfloat16 or wider, within the bound.
A program may use at most 64 MiB of HBM per device.

v0:
```python
import math

import jax
import jax.numpy as jnp
from jax import lax
from jax.sharding import PartitionSpec as P

HEADS1 = 8
HEADS2 = 16
WIN_LEVELS = 2
WIN_ROWS = 6
WIN_COLS = 12


EPSILON = 1e-05


def from_behind(block, axis, distance):
    devices = range(lax.axis_size(axis))
    route = [((i - distance) % len(devices), i) for i in devices]
    return lax.ppermute(block, axis, route)


def normalized(values):
    widened = values.astype(jnp.float32)
    center = jnp.mean(widened, axis=-1, keepdims=True)
    spread = jnp.mean(jnp.square(widened - center), axis=-1, keepdims=True)
    return ((widened - center) * lax.rsqrt(spread + EPSILON)).astype(jnp.bfloat16)


def window_softmax(queries, keys, values, labels, heads):
    levels, rows, columns, width = queries.shape
    stacks = levels // WIN_LEVELS
    across = columns // WIN_COLS
    head_size = width // heads

    def windows(array):
        shaped = array.reshape(stacks, WIN_LEVELS, rows, across, WIN_COLS, heads, head_size)
        shaped = shaped.transpose(0, 3, 1, 2, 4, 5, 6)
        return shaped.reshape(stacks * across, WIN_LEVELS * rows * WIN_COLS, heads, head_size)

    marks = labels.reshape(stacks, WIN_LEVELS, rows, across, WIN_COLS).transpose(0, 3, 1, 2, 4)
    marks = marks.reshape(stacks * across, WIN_LEVELS * rows * WIN_COLS)
    scores = jnp.einsum(
        "wqhd,wkhd->whqk", windows(queries), windows(keys), preferred_element_type=jnp.float32
    )
    scores = scores / math.sqrt(head_size)
    allowed = marks[:, None, :, None] == marks[:, None, None, :]
    scores = jnp.where(allowed, scores, -1e30)
    highest = jnp.max(scores, axis=-1, keepdims=True)
    expos = jnp.exp(scores - highest)
    weights = (expos / jnp.sum(expos, axis=-1, keepdims=True)).astype(jnp.bfloat16)
    mixed = jnp.einsum(
        "whqk,wkhd->wqhd", weights, windows(values), preferred_element_type=jnp.float32
    )
    mixed = mixed.astype(jnp.bfloat16)
    mixed = mixed.reshape(stacks, across, WIN_LEVELS, rows, WIN_COLS, width).transpose(
        0, 2, 3, 1, 4, 5
    )
    return mixed.reshape(levels, rows, columns, width)


def attend_bands(queries, keys, values, labels, heads):
    levels, rows, columns, width = queries.shape
    bands = rows // WIN_ROWS

    def by_band(array):
        return jnp.moveaxis(array.reshape((levels, bands, WIN_ROWS) + array.shape[2:]), 1, 0)

    def one_band(group):
        return window_softmax(group[0], group[1], group[2], group[3], heads)

    result = lax.map(one_band, (by_band(queries), by_band(keys), by_band(values), by_band(labels)))
    return jnp.moveaxis(result, 0, 1).reshape(levels, rows, columns, width)


def shifted_layer(field, labels, qkv_product, out_product, heads):
    levels, height, breadth, width = field.shape
    half_rows = WIN_ROWS // 2
    half_cols = WIN_COLS // 2
    marks = labels.astype(jnp.bfloat16)
    below = from_behind((field[:, :half_rows], marks[:, :half_rows]), "lat", -1)
    moved = jnp.concatenate([field[:, half_rows:], below[0]], axis=1)
    moved_marks = jnp.concatenate([marks[:, half_rows:], below[1]], axis=1)
    beside = from_behind((moved[:, :, :half_cols], moved_marks[:, :, :half_cols]), "lon", -1)
    moved = jnp.concatenate([moved[:, :, half_cols:], beside[0]], axis=2)
    moved_marks = jnp.concatenate([moved_marks[:, :, half_cols:], beside[1]], axis=2)
    packed = qkv_product(normalized(moved).reshape(-1, width)).astype(jnp.bfloat16)
    packed = packed.reshape(levels, height, breadth, 3 * width)
    mixed = attend_bands(
        packed[..., :width],
        packed[..., width : 2 * width],
        packed[..., 2 * width :],
        moved_marks.astype(jnp.int32),
        heads,
    )
    update = out_product(mixed.reshape(-1, width)).reshape(field.shape)
    result = (moved.astype(jnp.float32) + update).astype(jnp.bfloat16)
    returned = from_behind(result[:, :, breadth - half_cols :], "lon", 1)
    result = jnp.concatenate([returned, result[:, :, : breadth - half_cols]], axis=2)
    returned = from_behind(result[:, height - half_rows :], "lat", 1)
    return jnp.concatenate([returned, result[:, : height - half_rows]], axis=1)


def edge_labels(ids):
    height = ids.shape[1]
    global_rows = lax.axis_index("lat") * height + jnp.arange(height)
    edge = (global_rows < WIN_ROWS // 2).astype(jnp.int32)
    return ids * 2 + edge[None, :, None]


def merge_patches(field):
    levels, height, breadth, width = field.shape
    shaped = field.reshape(levels, height // 2, 2, breadth // 2, 2, width).transpose(
        0, 1, 3, 4, 2, 5
    )
    return shaped.reshape(levels, height // 2, breadth // 2, 4 * width)


def add_rows(left, piece):
    return jnp.dot(left, piece, preferred_element_type=jnp.float32)


def per_device(
    tokens, level_ids, coarse_ids, first_qkv, first_out, merge_weight, second_qkv, second_out
):

    def second_qkv_product(left):
        return add_rows(left, lax.all_gather(second_qkv, "lon", axis=0, tiled=True))

    def second_out_product(left):
        return add_rows(left, lax.all_gather(second_out, "lon", axis=0, tiled=True))

    def first_qkv_product(left):
        return jnp.dot(left, first_qkv, preferred_element_type=jnp.float32)

    def first_out_product(left):
        return jnp.dot(left, first_out, preferred_element_type=jnp.float32)

    skip = shifted_layer(
        tokens, edge_labels(level_ids), first_qkv_product, first_out_product, HEADS1
    )
    joined = merge_patches(skip)
    levels, height, breadth, width = joined.shape
    left = normalized(joined).reshape(-1, width)
    merged = add_rows(left, lax.all_gather(merge_weight, "lon", axis=0, tiled=True)).astype(
        jnp.bfloat16
    )
    merged = merged.reshape(levels, height, breadth, merge_weight.shape[1])
    coarse = shifted_layer(
        merged, edge_labels(coarse_ids), second_qkv_product, second_out_product, HEADS2
    )
    return (skip, coarse)


def solution(mesh):
    placed = (
        P(None, "lat", "lon", None),
        P(None, "lat", "lon"),
        P(None, "lat", "lon"),
        P(),
        P(),
        P("lon", None),
        P("lon", None),
        P("lon", None),
    )
    return jax.shard_map(
        per_device,
        mesh=mesh,
        in_specs=placed,
        out_specs=(P(None, "lat", "lon", None), P(None, "lat", "lon", None)),
        check_vma=False,
    )
```

profile of v0, /device:TPU:1, one launch (start us, length us, event | category | flops | bytes accessed | tf_op | source)
XLA Modules:
  0.0 254.0 jit_solution(9518751686207802184)
XLA Ops:
  9.6 8.4 %collective-permute-start = (bf16[2,3,24,512]{3,2,1,0:T(8,128)(2,1)S(1)}, bf16[2,3,24,512]{3,2,1,0:T(8,128)(2,1)S(1)}, u32[]{:S(2)}, u32[]{:S(2)}) collective-permute-start(bf16[2,3,24,512]{3,2,1,0:T(8,128)(2,1)S(1)} %slice.91), channel_id=1, source_target_pairs={{32,0},{64,32},{96,64},{128,96},{160,128},{192,160},{224,192},{256... | collective-permute-start | bytes 442376 | tf_op jit(solution)/shard_map/ppermute | solution.py:21
  22.1 2.6 %collective-permute-done.2 = bf16[2,3,24]{2,0,1:T(2,128)(2,1)S(1)} collective-permute-done((bf16[2,3,24]{2,0,1:T(2,128)(2,1)S(1)}, bf16[2,3,24]{2,0,1:T(2,128)(2,1)S(1)}, u32[]{:S(2)}, u32[]{:S(2)}) %collective-permute-start.2) | collective-permute-done | bytes 320 | tf_op jit(solution)/shard_map/ppermute | solution.py:21
  24.7 4.0 %collective-permute-start.3 = (bf16[2,12,6]{2,0,1:T(2,128)(2,1)S(1)}, bf16[2,12,6]{2,0,1:T(2,128)(2,1)S(1)}, u32[]{:S(2)}, u32[]{:S(2)}) collective-permute-start(bf16[2,12,6]{2,0,1:T(2,128)(2,1)S(1)} %pad_maximum_fusion.7), channel_id=1, source_target_pairs={{1,0},{2,1},{3,2},{4,3},{5,4},{6,5},{7,6},{8,7},{9,8},{10,9},{11,1... | collective-permute-start | bytes 872 | tf_op jit(solution)/shard_map/ppermute | solution.py:21
  28.8 9.0 %collective-permute-start.1 = (bf16[2,12,6,512]{3,2,1,0:T(8,128)(2,1)S(1)}, bf16[2,12,6,512]{3,2,1,0:T(8,128)(2,1)S(1)}, u32[]{:S(2)}, u32[]{:S(2)}) collective-permute-start(bf16[2,12,6,512]{3,2,1,0:T(8,128)(2,1)S(1)} %pad_maximum_fusion.5), channel_id=1, source_target_pairs={{1,0},{2,1},{3,2},{4,3},{5,4},{6,5},{7,6},{8,7},{9,8},{10,9},{11,1... | collective-permute-start | bytes 442376 | tf_op jit(solution)/shard_map/ppermute | solution.py:21
  42.0 21.8 %while.2 = (s32[]{:T(128)}, bf16[2,2,6,24,512]{4,3,2,0,1:T(8,128)(2,1)}, bf16[2,2,6,24,512]{4,3,2,0,1:T(8,128)(2,1)}, s32[2,2,6,24]{3,1,2,0:T(2,128)S(1)}, bf16[...) while((s32[]{:T(128)}, bf16[2,2,6,24,512]{4,3,2,0,1:T(8,128)(2,1)}, ...), condition=%wide.region_5.6_spmd, body=%wide.region_2.5_spmd.sunk | while | flops 87114384 | bytes 23410532 | solution.py:73
  44.9 3.6 %fusion.99 = (f32[2,8,144]{2,1,0:T(8,128)S(1)}, f32[2,8,144,144]{2,3,1,0:T(8,128)}) fusion(pred[2,144,144]{1,2,0:T(8,128)(4,1)S(1)} %broadcast_compare_fusion.3, bf16[2,144,8,64]{3,2,1,0:T(8,128)(2,1)S(1)} %bitcast.117, bf16[2,144,8,64]{3,2,1,0:T(8,128)(2,1)} %bitcast.118), kind=kOutput, calls=%fused_computation.98.clone.1 | convolution fusion | flops 43794576 | bytes 1967616 | tf_op jit(solution)/shard_map/while/body/eval_jaxpr/sub | solution.py:51
  55.9 3.6 %fusion.99 = (f32[2,8,144]{2,1,0:T(8,128)S(1)}, f32[2,8,144,144]{2,3,1,0:T(8,128)}) fusion(pred[2,144,144]{1,2,0:T(8,128)(4,1)S(1)} %broadcast_compare_fusion.3, bf16[2,144,8,64]{3,2,1,0:T(8,128)(2,1)S(1)} %bitcast.117, bf16[2,144,8,64]{3,2,1,0:T(8,128)(2,1)} %bitcast.118), kind=kOutput, calls=%fused_computation.98.clone.1 | convolution fusion | flops 43794576 | bytes 1967616 | tf_op jit(solution)/shard_map/while/body/eval_jaxpr/sub | solution.py:51
  67.9 5.0 %collective-permute-done.4 = bf16[2,12,6,512]{3,2,1,0:T(8,128)(2,1)S(1)} collective-permute-done((bf16[2,12,6,512]{3,2,1,0:T(8,128)(2,1)S(1)}, bf16[2,12,6,512]{3,2,1,0:T(8,128)(2,1)S(1)}, u32[]{:S(2)}, u32[]{:S(2)}) %collective-permute-start.4) | collective-permute-done | bytes 147488 | tf_op jit(solution)/shard_map/ppermute | solution.py:21
  72.9 3.8 %collective-permute-start.5 = (bf16[2,3,24,512]{3,2,1,0:T(8,128)(2,1)S(1)}, bf16[2,3,24,512]{3,2,1,0:T(8,128)(2,1)S(1)}, u32[]{:S(2)}, u32[]{:S(2)}) collective-permute-start(bf16[2,3,24,512]{3,2,1,0:T(8,128)(2,1)S(1)} %pad_maximum_fusion.6), channel_id=1, source_target_pairs={{480,0},{0,32},{32,64},{64,96},{96,128},{128,160},{160,192},{192,2... | collective-permute-start | bytes 442376 | tf_op jit(solution)/shard_map/ppermute | solution.py:21
  76.7 5.3 %collective-permute-start.8 = (bf16[2,3,12]{2,0,1:T(2,128)(2,1)S(1)}, bf16[2,3,12]{2,0,1:T(2,128)(2,1)S(1)}, u32[]{:S(2)}, u32[]{:S(2)}) collective-permute-start(bf16[2,3,12]{2,0,1:T(2,128)(2,1)S(1)} %get-tuple-element.94), channel_id=1, source_target_pairs={{32,0},{64,32},{96,64},{128,96},{160,128},{192,160},{224,192},{256... | collective-permute-start | bytes 440 | tf_op jit(solution)/shard_map/ppermute | solution.py:21
  87.9 2.3 reshape.293
  90.3 3.0 %convolution_convert_fusion.4 = bf16[144,1024]{1,0:T(8,128)(2,1)S(1)} fusion(bf16[2048,1024]{1,0:T(8,128)(2,1)} %all-gather.4.cloned.1.call-done, f32[144,2048]{1,0:T(8,128)S(1)} %reshape.293, f32[144]{0:T(256)S(1)} %rsqrt.36, f32[144]{0:T(256)S(1)} %div.56), kind=kOutput, calls=%fused_computation.37 | convolution fusion | flops 605011968 | bytes 5670016 | tf_op jit(solution)/shard_map/dot_general | solution.py:121
  93.4 6.7 %collective-permute-start.6 = (bf16[2,3,12,1024]{3,2,1,0:T(8,128)(2,1)S(1)}, bf16[2,3,12,1024]{3,2,1,0:T(8,128)(2,1)S(1)}, u32[]{:S(2)}, u32[]{:S(2)}) collective-permute-start(bf16[2,3,12,1024]{3,2,1,0:T(8,128)(2,1)S(1)} %get-tuple-element.90), channel_id=1, source_target_pairs={{32,0},{64,32},{96,64},{128,96},{160,128},{192,160},{224,192},{256... | collective-permute-start | bytes 442376 | tf_op jit(solution)/shard_map/ppermute | solution.py:21
  100.2 7.7 %collective-permute-start.9 = (bf16[2,6,6]{2,0,1:T(2,128)(2,1)S(1)}, bf16[2,6,6]{2,0,1:T(2,128)(2,1)S(1)}, u32[]{:S(2)}, u32[]{:S(2)}) collective-permute-start(bf16[2,6,6]{2,0,1:T(2,128)(2,1)S(1)} %get-tuple-element.92), channel_id=1, source_target_pairs={{1,0},{2,1},{3,2},{4,3},{5,4},{6,5},{7,6},{8,7},{9,8},{10,9},{11,1... | collective-permute-start | bytes 440 | tf_op jit(solution)/shard_map/ppermute | solution.py:21
  109.0 8.0 %collective-permute-start.7 = (bf16[2,6,6,1024]{3,2,1,0:T(8,128)(2,1)S(1)}, bf16[2,6,6,1024]{3,2,1,0:T(8,128)(2,1)S(1)}, u32[]{:S(2)}, u32[]{:S(2)}) collective-permute-start(bf16[2,6,6,1024]{3,2,1,0:T(8,128)(2,1)S(1)} %get-tuple-element.88), channel_id=1, source_target_pairs={{1,0},{2,1},{3,2},{4,3},{5,4},{6,5},{7,6},{8,7},{9,8},{10,9},{11,1... | collective-permute-start | bytes 442376 | tf_op jit(solution)/shard_map/ppermute | solution.py:21
  118.9 41.2 %all-gather.6.cloned.1.call-done = bf16[1024,3072]{1,0:T(8,128)(2,1)} async-done(((bf16[32,3072]{1,0:T(8,128)(2,1)}), bf16[1024,3072]{1,0:T(8,128)(2,1)}) %all-gather.6.cloned.1.call-update) | async-done | bytes 6291472 | tf_op jit(solution)/shard_map/all_gather | solution.py:129
  160.1 4.9 %convolution_convert_fusion.1 = bf16[144,3072]{1,0:T(8,128)(2,1)} fusion(bf16[1024,3072]{1,0:T(8,128)(2,1)} %all-gather.6.cloned.1.call-done, f32[144,1024]{1,0:T(8,128)S(1)} %reshape.294, f32[144]{0:T(256)S(1)} %rsqrt.38, f32[144]{0:T(256)S(1)} %div.59), kind=kOutput, calls=%fused_computation.23 | convolution fusion | flops 906854400 | bytes 7767168 | tf_op jit(solution)/shard_map/dot_general | solution.py:121
  171.2 3.6 %fusion.80 = (f32[16,144]{1,0:T(8,128)S(1)}, f32[16,144,144]{1,2,0:T(8,128)}) fusion(pred[144,144]{0,1:T(8,128)(4,1)S(1)} %copy-done.12, bf16[144,16,64]{2,1,0:T(8,128)(2,1)} %reshape.291, bf16[144,16,64]{2,1,0:T(8,128)(2,1)S(1)} %reshape.290), kind=kOutput, calls=%fused_computation.104 | convolution fusion | flops 43794576 | bytes 1946880 | tf_op jit(solution)/shard_map/while/body/eval_jaxpr/sub | solution.py:51
  174.8 3.0 %fusion.35 = bf16[1,144,16,64]{1,3,2,0:T(8,128)(2,1)} fusion(f32[16,144,144]{1,2,0:T(8,128)} %get-tuple-element.96, f32[16,144]{1,0:T(8,128)S(1)} %get-tuple-element.95, bf16[144,16,64]{2,1,0:T(8,128)(2,1)S(1)} %copy-done.11), kind=kOutput, calls=%fused_computation.36 | convolution fusion | flops 43278336 | bytes 1926144 | tf_op jit(solution)/shard_map/while/body/eval_jaxpr/whqk,wkhd->wqhd/dot_general | solution.py:53
  179.8 49.0 %all-gather.8.cloned.1.call-done = bf16[1024,1024]{1,0:T(8,128)(2,1)} async-done(((bf16[32,1024]{1,0:T(8,128)(2,1)}), bf16[1024,1024]{1,0:T(8,128)(2,1)}) %all-gather.8.cloned.1.call-update) | async-done | bytes 2097168 | tf_op jit(solution)/shard_map/all_gather | solution.py:132
  231.0 2.6 %collective-permute-start.10 = (bf16[2,6,6,1024]{3,2,1,0:T(8,128)(2,1)S(1)}, bf16[2,6,6,1024]{3,2,1,0:T(8,128)(2,1)S(1)}, u32[]{:S(2)}, u32[]{:S(2)}) collective-permute-start(bf16[2,6,6,1024]{3,2,1,0:T(8,128)(2,1)S(1)} %get-tuple-element.85), channel_id=1, source_target_pairs={{31,0},{0,1},{1,2},{2,3},{3,4},{4,5},{5,6},{6,7},{7,8},{8,9},{9,10... | collective-permute-start | bytes 442376 | tf_op jit(solution)/shard_map/ppermute | solution.py:21
  233.6 2.6 %collective-permute-done.10 = bf16[2,6,6,1024]{3,2,1,0:T(8,128)(2,1)S(1)} collective-permute-done((bf16[2,6,6,1024]{3,2,1,0:T(8,128)(2,1)S(1)}, bf16[2,6,6,1024]{3,2,1,0:T(8,128)(2,1)S(1)}, u32[]{:S(2)}, u32[]{:S(2)}) %collective-permute-start.10) | collective-permute-done | bytes 147488 | tf_op jit(solution)/shard_map/ppermute | solution.py:21
  236.3 4.4 %collective-permute-start.11 = (bf16[2,3,12,1024]{3,2,1,0:T(8,128)(2,1)S(1)}, bf16[2,3,12,1024]{3,2,1,0:T(8,128)(2,1)S(1)}, u32[]{:S(2)}, u32[]{:S(2)}) collective-permute-start(bf16[2,3,12,1024]{3,2,1,0:T(8,128)(2,1)S(1)} %fusion.52), channel_id=1, source_target_pairs={{480,0},{0,32},{32,64},{64,96},{96,128},{128,160},{160,192},{192,2... | collective-permute-start | bytes 442376 | tf_op jit(solution)/shard_map/ppermute | solution.py:21
  240.8 5.6 %collective-permute-done.11 = bf16[2,3,12,1024]{3,2,1,0:T(8,128)(2,1)S(1)} collective-permute-done((bf16[2,3,12,1024]{3,2,1,0:T(8,128)(2,1)S(1)}, bf16[2,3,12,1024]{3,2,1,0:T(8,128)(2,1)S(1)}, u32[]{:S(2)}, u32[]{:S(2)}) %collective-permute-start.11) | collective-permute-done | bytes 147488 | tf_op jit(solution)/shard_map/ppermute | solution.py:21
  (155 shorter events, 49.7 us)
Async XLA Ops:
  7.2 32.8 %copy-start = (bf16[512,1536]{1,0:T(8,128)(2,1)S(1)}, bf16[512,1536]{1,0:T(8,128)(2,1)}, u32[]{:S(2)}) copy-start(bf16[512,1536]{1,0:T(8,128)(2,1)} %param.13) | copy-start | bytes 4718596
  7.2 83.1 %all-gather.4.cloned.1.call-start = ((), (), s32[]{:S(2)}) async-start(), calls=%async_computation | async-start | bytes 4325376 | tf_op jit(solution)/shard_map/all_gather | solution.py:146
  7.9 152.1 %all-gather.6.cloned.1.call-start = ((), (), s32[]{:S(2)}) async-start(), calls=%async_computation.1 | async-start | bytes 6488064 | tf_op jit(solution)/shard_map/all_gather | solution.py:129
  8.7 220.1 %all-gather.8.cloned.1.call-start = ((), (), s32[]{:S(2)}) async-start(), calls=%async_computation.2 | async-start | bytes 2162688 | tf_op jit(solution)/shard_map/all_gather | solution.py:132
  9.6 19.2 %collective-permute-start = (bf16[2,3,24,512]{3,2,1,0:T(8,128)(2,1)S(1)}, bf16[2,3,24,512]{3,2,1,0:T(8,128)(2,1)S(1)}, u32[]{:S(2)}, u32[]{:S(2)}) collective-permute-start(bf16[2,3,24,512]{3,2,1,0:T(8,128)(2,1)S(1)} %slice.91), channel_id=1, source_target_pairs={{32,0},{64,32},{96,64},{128,96},{160,128},{192,160},{224,192},{256... | collective-permute-start | bytes 442376 | tf_op jit(solution)/shard_map/ppermute | solution.py:21
  18.8 5.8 %collective-permute-start.2 = (bf16[2,3,24]{2,0,1:T(2,128)(2,1)S(1)}, bf16[2,3,24]{2,0,1:T(2,128)(2,1)S(1)}, u32[]{:S(2)}, u32[]{:S(2)}) collective-permute-start(bf16[2,3,24]{2,0,1:T(2,128)(2,1)S(1)} %slice.124), channel_id=1, source_target_pairs={{32,0},{64,32},{96,64},{128,96},{160,128},{192,160},{224,192},{256... | collective-permute-start | bytes 872 | tf_op jit(solution)/shard_map/ppermute | solution.py:21
  24.7 13.1 %collective-permute-start.3 = (bf16[2,12,6]{2,0,1:T(2,128)(2,1)S(1)}, bf16[2,12,6]{2,0,1:T(2,128)(2,1)S(1)}, u32[]{:S(2)}, u32[]{:S(2)}) collective-permute-start(bf16[2,12,6]{2,0,1:T(2,128)(2,1)S(1)} %pad_maximum_fusion.7), channel_id=1, source_target_pairs={{1,0},{2,1},{3,2},{4,3},{5,4},{6,5},{7,6},{8,7},{9,8},{10,9},{11,1... | collective-permute-start | bytes 872 | tf_op jit(solution)/shard_map/ppermute | solution.py:21
  28.8 10.0 %collective-permute-start.1 = (bf16[2,12,6,512]{3,2,1,0:T(8,128)(2,1)S(1)}, bf16[2,12,6,512]{3,2,1,0:T(8,128)(2,1)S(1)}, u32[]{:S(2)}, u32[]{:S(2)}) collective-permute-start(bf16[2,12,6,512]{3,2,1,0:T(8,128)(2,1)S(1)} %pad_maximum_fusion.5), channel_id=1, source_target_pairs={{1,0},{2,1},{3,2},{4,3},{5,4},{6,5},{7,6},{8,7},{9,8},{10,9},{11,1... | collective-permute-start | bytes 442376 | tf_op jit(solution)/shard_map/ppermute | solution.py:21
  38.1 1.9 copy-start.1
  44.9 3.6 %copy-start.6 = (bf16[2,2,6,24,512]{4,3,2,0,1:T(8,128)(2,1)S(1)}, bf16[2,2,6,24,512]{4,3,2,0,1:T(8,128)(2,1)}, u32[]{:S(2)}) copy-start(bf16[2,2,6,24,512]{4,3,2,0,1:T(8,128)(2,1)} %get-tuple-element.158) | copy-start | bytes 1769476 | tf_op jit(solution)/shard_map/while
  55.9 3.6 %copy-start.6 = (bf16[2,2,6,24,512]{4,3,2,0,1:T(8,128)(2,1)S(1)}, bf16[2,2,6,24,512]{4,3,2,0,1:T(8,128)(2,1)}, u32[]{:S(2)}) copy-start(bf16[2,2,6,24,512]{4,3,2,0,1:T(8,128)(2,1)} %get-tuple-element.158) | copy-start | bytes 1769476 | tf_op jit(solution)/shard_map/while
  63.9 3.9 %copy-start.13 = (s32[2,6,12]{2,0,1:T(2,128)S(1)}, s32[2,6,12]{2,0,1:T(2,128)}, u32[]{:S(2)}) copy-start(s32[2,6,12]{2,0,1:T(2,128)} %param.12) | copy-start | bytes 1732
  65.9 7.0 %collective-permute-start.4 = (bf16[2,12,6,512]{3,2,1,0:T(8,128)(2,1)S(1)}, bf16[2,12,6,512]{3,2,1,0:T(8,128)(2,1)S(1)}, u32[]{:S(2)}, u32[]{:S(2)}) collective-permute-start(bf16[2,12,6,512]{3,2,1,0:T(8,128)(2,1)S(1)} %slice.129), channel_id=1, source_target_pairs={{31,0},{0,1},{1,2},{2,3},{3,4},{4,5},{5,6},{6,7},{7,8},{8,9},{9,10... | collective-permute-start | bytes 442376 | tf_op jit(solution)/shard_map/ppermute | solution.py:21
  72.9 9.6 %collective-permute-start.5 = (bf16[2,3,24,512]{3,2,1,0:T(8,128)(2,1)S(1)}, bf16[2,3,24,512]{3,2,1,0:T(8,128)(2,1)S(1)}, u32[]{:S(2)}, u32[]{:S(2)}) collective-permute-start(bf16[2,3,24,512]{3,2,1,0:T(8,128)(2,1)S(1)} %pad_maximum_fusion.6), channel_id=1, source_target_pairs={{480,0},{0,32},{32,64},{64,96},{96,128},{128,160},{160,192},{192,2... | collective-permute-start | bytes 442376 | tf_op jit(solution)/shard_map/ppermute | solution.py:21
  76.7 23.4 %collective-permute-start.8 = (bf16[2,3,12]{2,0,1:T(2,128)(2,1)S(1)}, bf16[2,3,12]{2,0,1:T(2,128)(2,1)S(1)}, u32[]{:S(2)}, u32[]{:S(2)}) collective-permute-start(bf16[2,3,12]{2,0,1:T(2,128)(2,1)S(1)} %get-tuple-element.94), channel_id=1, source_target_pairs={{32,0},{64,32},{96,64},{128,96},{160,128},{192,160},{224,192},{256... | collective-permute-start | bytes 440 | tf_op jit(solution)/shard_map/ppermute | solution.py:21
  82.7 1.8 copy-start.7
  93.4 15.5 %collective-permute-start.6 = (bf16[2,3,12,1024]{3,2,1,0:T(8,128)(2,1)S(1)}, bf16[2,3,12,1024]{3,2,1,0:T(8,128)(2,1)S(1)}, u32[]{:S(2)}, u32[]{:S(2)}) collective-permute-start(bf16[2,3,12,1024]{3,2,1,0:T(8,128)(2,1)S(1)} %get-tuple-element.90), channel_id=1, source_target_pairs={{32,0},{64,32},{96,64},{128,96},{160,128},{192,160},{224,192},{256... | collective-permute-start | bytes 442376 | tf_op jit(solution)/shard_map/ppermute | solution.py:21
  100.2 8.6 %collective-permute-start.9 = (bf16[2,6,6]{2,0,1:T(2,128)(2,1)S(1)}, bf16[2,6,6]{2,0,1:T(2,128)(2,1)S(1)}, u32[]{:S(2)}, u32[]{:S(2)}) collective-permute-start(bf16[2,6,6]{2,0,1:T(2,128)(2,1)S(1)} %get-tuple-element.92), channel_id=1, source_target_pairs={{1,0},{2,1},{3,2},{4,3},{5,4},{6,5},{7,6},{8,7},{9,8},{10,9},{11,1... | collective-permute-start | bytes 440 | tf_op jit(solution)/shard_map/ppermute | solution.py:21
  109.0 8.9 %collective-permute-start.7 = (bf16[2,6,6,1024]{3,2,1,0:T(8,128)(2,1)S(1)}, bf16[2,6,6,1024]{3,2,1,0:T(8,128)(2,1)S(1)}, u32[]{:S(2)}, u32[]{:S(2)}) collective-permute-start(bf16[2,6,6,1024]{3,2,1,0:T(8,128)(2,1)S(1)} %get-tuple-element.88), channel_id=1, source_target_pairs={{1,0},{2,1},{3,2},{4,3},{5,4},{6,5},{7,6},{8,7},{9,8},{10,9},{11,1... | collective-permute-start | bytes 442376 | tf_op jit(solution)/shard_map/ppermute | solution.py:21
  168.7 2.4 copy-start.12
  171.2 3.6 %copy-start.11 = (bf16[144,16,64]{2,1,0:T(8,128)(2,1)S(1)}, bf16[144,16,64]{2,1,0:T(8,128)(2,1)}, u32[]{:S(2)}) copy-start(bf16[144,16,64]{2,1,0:T(8,128)(2,1)} %reshape.289) | copy-start | bytes 884740
  177.7 51.0 %copy-start.9 = (bf16[2,6,6,1024]{3,2,1,0:T(8,128)(2,1)S(1)}, bf16[2,6,6,1024]{3,2,1,0:T(8,128)(2,1)}, u32[]{:S(2)}) copy-start(bf16[2,6,6,1024]{3,2,1,0:T(8,128)(2,1)} %copy-done.8) | copy-start | bytes 442372
  231.0 5.2 %collective-permute-start.10 = (bf16[2,6,6,1024]{3,2,1,0:T(8,128)(2,1)S(1)}, bf16[2,6,6,1024]{3,2,1,0:T(8,128)(2,1)S(1)}, u32[]{:S(2)}, u32[]{:S(2)}) collective-permute-start(bf16[2,6,6,1024]{3,2,1,0:T(8,128)(2,1)S(1)} %get-tuple-element.85), channel_id=1, source_target_pairs={{31,0},{0,1},{1,2},{2,3},{3,4},{4,5},{5,6},{6,7},{7,8},{8,9},{9,10... | collective-permute-start | bytes 442376 | tf_op jit(solution)/shard_map/ppermute | solution.py:21
  236.3 10.0 %collective-permute-start.11 = (bf16[2,3,12,1024]{3,2,1,0:T(8,128)(2,1)S(1)}, bf16[2,3,12,1024]{3,2,1,0:T(8,128)(2,1)S(1)}, u32[]{:S(2)}, u32[]{:S(2)}) collective-permute-start(bf16[2,3,12,1024]{3,2,1,0:T(8,128)(2,1)S(1)} %fusion.52), channel_id=1, source_target_pairs={{480,0},{0,32},{32,64},{64,96},{96,128},{128,160},{160,192},{192,2... | collective-permute-start | bytes 442376 | tf_op jit(solution)/shard_map/ppermute | solution.py:21
  (10 other events, 11.2 us)
Sparse Core Ops, SparseCore 0:
  10.1 75.5 all-gather.3
  87.8 72.1 all-gather.5
  162.2 66.5 all-gather.7
where the time goes:
time: 258 us; the launch traced here: 254 us
  waiting for transfers between devices  110 us (43%)
  starting transfers between devices  64.1 us (25%)
  matrix products  31 us (12%)
  local copies, waits for them, and re-layouts  28.2 us (11%)
  between operations  14.3 us (6%)
  other arithmetic  6.58 us (3%)
    ppermute x12, starting transfers between devices, from_behind(): return lax.ppermute(block, axis, route)  64 us
    all_gather x1, waiting for transfers between devices, second_out_product(): return add_rows(left, lax.all_gather(second_out, 'lon', axis=0, tiled=True))  49 us
    all_gather x1, waiting for transfers between devices, second_qkv_product(): return add_rows(left, lax.all_gather(second_qkv, 'lon', axis=0, tiled=True))  41.2 us
    ppermute x12, waiting for transfers between devices, from_behind(): return lax.ppermute(block, axis, route)  18 us
    sub x3, matrix products, window_softmax(): expos = jnp.exp(scores - highest)  10.7 us
    dot_general x3, matrix products, add_rows(): return jnp.dot(left, piece, preferred_element_type=jnp.float32)  10.1 us
    dot_general x3, matrix products, window_softmax(): jnp.einsum('whqk,wkhd->wqhd', weights, windows(values), preferred_element...  7.14 us
  transfers between devices with their start and end apart: 15, of which 10 were waited for; matrix products, arithmetic and copies ran while one was open for 24% of the time, Pallas kernels for 0%

commit v1 on v0

v1 whole, which is shorter than its diff:
```python
import functools

import jax
import jax.numpy as jnp
import numpy as np
from jax import lax
from jax.experimental import pallas as pl
from jax.experimental.pallas import tpu as pltpu
from jax.sharding import PartitionSpec as P

EPSILON = 1e-05
QUAD = 40
TOKENS = 4 * QUAD
GROUP = 4
HEAD = 64
MESH = pl.DeviceIdType.MESH
F32 = jnp.float32
BF16 = jnp.bfloat16


def one_hot_tables():
    pick = np.zeros((2, TOKENS, 288), np.float32)
    merge = np.zeros((TOKENS, TOKENS), np.float32)
    expand = np.zeros((144, TOKENS), np.float32)
    expand2 = np.zeros((96, 2 * QUAD), np.float32)
    tile = np.zeros((TOKENS, GROUP * TOKENS), np.float32)
    marks = np.zeros((TOKENS, 4 * 192), np.float32)
    for level in range(2):
        for r in range(3):
            for c in range(6):
                at = level * 18 + r * 6 + c
                for q in range(4):
                    rh, ch = divmod(q, 2)
                    row = q * QUAD + at
                    for w in range(2):
                        col = level * 144 + (rh * 3 + r) * 24 + 6 + 4 * w + ch * 6 + c
                        pick[w, row, col] = 1
                    fr, fc = 2 * r + q % 2, 2 * c + q // 2
                    sub = (fr // 3) * 2 + fc // 6
                    merge[row, sub * QUAD + level * 18 + (fr % 3) * 6 + fc % 6] = 1
                    expand[level * 72 + r * 24 + q * 6 + c, row] = 1
                    source = rh * 2 + ch
                    r_in, c_in = (r + 3 if rh == 0 else r), (c + 6 if ch == 0 else c)
                    marks[row, source * 192 + level * 96 + r_in * 16 + c_in] = 1
                for q in range(2):
                    expand2[(level * 3 + r) * 16 + q * 6 + c, q * QUAD + at] = 1
    for h in range(GROUP):
        tile[np.arange(TOKENS), h * TOKENS + np.arange(TOKENS)] = 1
    return [t.astype(BF16) for t in (pick, merge, expand, expand2, tile, marks)]


def dot(a, b, dims=((1,), (0,))):
    return lax.dot_general(a, b, (dims, ((), ())), preferred_element_type=F32)


def normalized(x):
    center = jnp.mean(x, axis=-1, keepdims=True)
    x = x - center
    spread = jnp.mean(x * x, axis=-1, keepdims=True)
    return (x * lax.rsqrt(spread + EPSILON)).astype(BF16)


def score_bias(marks, tile):
    across = dot(marks, tile, ((0,), (0,)))
    keys = marks.astype(F32)[:, :1]
    return jnp.where(keys == across[:1, :], 0.0, -1e30).astype(F32)


def attend(q, k, v, bias):
    lane = lax.broadcasted_iota(jnp.int32, (TOKENS, GROUP * HEAD), 1)
    scaled = q * BF16(0.125)
    zero = jnp.zeros_like(q)
    stacked = jnp.concatenate(
        [jnp.where(lane // HEAD == h, scaled, zero) for h in range(GROUP)], axis=0
    )
    scores = dot(k, stacked, ((1,), (1,))) + bias
    expos = jnp.exp(scores - jnp.max(scores, axis=0, keepdims=True)).astype(BF16)
    extended = jnp.concatenate([v, jnp.ones((TOKENS, 128), BF16)], axis=1)
    both = dot(expos, extended, ((0,), (0,)))
    part = lambda h: both[h * TOKENS : (h + 1) * TOKENS]
    halves = []
    for pair in range(2):
        first, second = part(2 * pair), part(2 * pair + 1)
        low = lane[:, :128] < HEAD
        at = slice(pair * 128, pair * 128 + 128)
        top = jnp.where(low, first[:, at], second[:, at])
        total = jnp.where(low, first[:, 256:], second[:, 256:])
        halves.append(top / total)
    return jnp.concatenate(halves, axis=1)


def kernel(
    sizes,
    tokens, lab1, lab2, first_qkv, first_out, merge_weight, second_qkv, second_out,
    pick, merge, expand, expand2, tile, marks,
    skip_out, coarse_out,
    X, L1, L2, WQ1, WO1, GW, PK, MX, OUTQ, FINE, SKQ, SK, MG, JN, PK2, MX2, COQ, CQ, CO,
    local_sem, halo_recv, mid_recv, skip_recv, back_recv, send_sem, gather_sem, sib_sem, drain_sem, out_sem,
):
    nlat, nlon = sizes
    lat, lon = lax.axis_index("lat"), lax.axis_index("lon")
    up, down = lax.rem(lat + nlat - 1, nlat), lax.rem(lat + 1, nlat)
    left, right = lax.rem(lon + nlon - 1, nlon), lax.rem(lon + 1, nlon)
    nz = nlon // 4
    z = lon // 4
    core = lax.rem(lon, 2)
    x_lo = lax.rem(lon // 2, 2)
    sibling = lon + 1 - 2 * core
    across = lon + 2 - 4 * x_lo
    other_lat = lat + 1 - 2 * lax.rem(lat, 2)
    z_next, z_prev = lax.rem(lon + 4, nlon), lax.rem(lon + nlon - 4, nlon)

    def local(src, dst, n):
        copy = pltpu.make_async_copy(src, dst, local_sem.at[n])
        copy.start()
        return copy

    own = [local(merge_weight, GW.at[lon, 0:64], 0)]
    for n in range(3):
        own.append(
            local(second_qkv.at[:, n * 1024 : (n + 1) * 1024], GW.at[lon, 64 + 32 * n : 96 + 32 * n], 1 + n)
        )
    own.append(local(second_out, GW.at[lon, 160:192], 4))
    mine = [
        local(tokens, X.at[:, 0:12, 0:24], 5),
        local(lab1, L1.at[:, 0:12, 0:24], 6),
        local(lab2, L2.at[0], 7),
        local(first_qkv, WQ1, 8),
        local(first_out, WO1, 9),
    ]

    barrier = pltpu.get_barrier_semaphore()
    partners = [
        (up, lon), (down, lon), (lat, left), (lat, right), (up, left), (down, right),
        (lat, z_next), (lat, z_prev), (lat, across), (other_lat, across), (lat, sibling),
    ]
    for partner in partners:
        pl.semaphore_signal(barrier, inc=1, device_id=partner, device_id_type=MESH)
    pl.semaphore_wait(barrier, len(partners))

    sends = []

    def send(src, dst, recv, to):
        copy = pltpu.make_async_remote_copy(
            src_ref=src, dst_ref=dst, send_sem=send_sem.at[len(sends)], recv_sem=recv,
            device_id=to, device_id_type=MESH,
        )
        copy.start()
        sends.append(copy)

    corners = [
        ((lat, left), slice(0, 12), slice(0, 8), slice(0, 12), slice(24, 32)),
        ((up, lon), slice(0, 3), slice(0, 24), slice(12, 15), slice(0, 24)),
        ((up, left), slice(0, 3), slice(0, 8), slice(12, 15), slice(24, 32)),
    ]
    for n, (to, r, c, r_to, c_to) in enumerate(corners):
        send(tokens.at[:, r, c], X.at[:, r_to, c_to], halo_recv.at[3 * n], to)
        send(lab1.at[:, r, c], L1.at[:, r_to, c_to], halo_recv.at[3 * n + 1], to)
        send(lab2, L2.at[n + 1], halo_recv.at[3 * n + 2], to)

    def await_halo(n):
        to, r, c, r_to, c_to = corners[n]
        for src, dst, s in (
            (tokens.at[:, r, c], X.at[:, r_to, c_to], 0),
            (lab1.at[:, r, c], L1.at[:, r_to, c_to], 1),
            (lab2, L2.at[n + 1], 2),
        ):
            pltpu.make_async_copy(dst, dst, halo_recv.at[3 * n + s]).wait()

    def piece(c, shard, first=0, rows=64):
        return GW.at[shard, 64 * c + first : 64 * c + first + rows]

    def forward(c, shard, to, recv, first=0, rows=64):
        ref = piece(c, shard, first, rows)
        pltpu.make_async_remote_copy(
            src_ref=ref, dst_ref=ref, send_sem=drain_sem.at[c], recv_sem=recv,
            device_id=to, device_id_type=MESH,
        ).start()

    def shard_at(step):
        return lax.rem(lon + 4 * step + nlon, nlon)

    def across_shard(shard):
        return shard + 2 - 4 * lax.rem(shard // 2, 2)

    def spread(c, shard):
        hop = lax.rem(shard // 4, 2)
        forward(c, shard, (lat + hop * (other_lat - lat), across), gather_sem.at[c, shard])
        forward(c, shard, (lat, sibling), sib_sem.at[c])

    def arrived(c, shard):
        ref = piece(c, shard)
        pltpu.make_async_copy(ref, ref, gather_sem.at[c, shard]).wait()

    half = nz // 2

    def gather_step(c, k):
        if k == 0:
            forward(c, lon, (lat, z_next), gather_sem.at[c, lon])
            forward(c, lon, (lat, z_prev), gather_sem.at[c, lon])
            spread(c, lon)
        elif k < half:
            behind, ahead = shard_at(-k), shard_at(k)
            arrived(c, behind)
            first = dict(first=0, rows=32) if k == half - 1 else {}
            forward(c, behind, (lat, z_next), gather_sem.at[c, behind], **first)
            arrived(c, ahead)
            second = dict(first=32, rows=32) if k == half - 1 else {}
            forward(c, ahead, (lat, z_prev), gather_sem.at[c, ahead], **second)
            spread(c, behind)
            spread(c, ahead)
        elif k == half:
            arrived(c, shard_at(half))
            spread(c, shard_at(half))
        k = k - 1
        if k >= 0:
            for step in sorted({k, -k} if k < half else {half}):
                shard = across_shard(shard_at(step))
                arrived(c, shard)
                forward(c, shard, (lat, sibling), sib_sem.at[c])

    def await_weights(c):
        ref = GW.at[0 : nlon // 2, 64 * c : 64 * c + 64]
        pltpu.make_async_copy(ref, ref, sib_sem.at[c]).wait()

    for copy in own:
        copy.wait()
    pending = []
    for c in range(3):
        pending += [(c, k) for k in range(half + 2)]
    order = [(0, 0), (1, 0)] + [(0, 1), (1, 1), (0, 2), (1, 2), (0, 3), (1, 3), (0, 4), (1, 4), (2, 0), (0, 5)]
    order += [(1, 5), (2, 1), (2, 2), (2, 3), (2, 4), (2, 5)]
    assert sorted(order) == sorted(pending)

    def service(n):
        for _ in range(n):
            if order:
                gather_step(*order.pop(0))

    service(2)
    for copy in mine:
        copy.wait()

    def spot(a, b):
        return ((a // 2) * 2 + b // 2) * 4 + (a % 2) * 2 + b % 2

    def window(b, w):
        r_at, c_at = slice(3 + 6 * b, 9 + 6 * b), slice(8 * w, 8 * w + 24)
        field = X[:, r_at, c_at].reshape(288, 512)
        labels = L1[:, r_at, c_at].reshape(288, 128)
        select = pick[w]
        rolled = dot(select, field)
        bias = score_bias(dot(select, labels).astype(BF16), tile[...])
        normed = normalized(rolled)
        for n in range(3):
            PK[:, 512 * n : 512 * n + 512] = dot(normed, WQ1[:, 512 * n : 512 * n + 512]).astype(BF16)
        for g in range(2):
            at = 256 * g
            mixed = attend(
                PK[:, at : at + 256], PK[:, 512 + at : 768 + at], PK[:, 1024 + at : 1280 + at], bias
            )
            MX[:, at : at + 256] = mixed.astype(BF16)
            if g == 0:
                service(1)
        update = rolled + dot(MX[...], WO1[...])
        for q in range(4):
            r, c = 2 * b + q // 2, 2 * w + q % 2
            value = update[q * QUAD : (q + 1) * QUAD].astype(BF16)
            OUTQ[4 * r + c] = value
            if r >= 1 and c >= 1:
                FINE[spot(r - 1, c - 1)] = value
            if r <= 2 and c <= 2:
                SKQ[4 * (r + 1) + c + 1] = value
        service(1)
        for q in range(4):
            r, c = 2 * b + q // 2, 2 * w + q % 2
            if r == 0 or c == 0:
                to = (lat if r else up, lon if c else left)
                at = spot(r - 1 if r else 3, c - 1 if c else 3)
                send(OUTQ.at[4 * r + c], FINE.at[at], mid_recv.at[at], to)
            if r == 3 or c == 3:
                to = (down if r == 3 else lat, right if c == 3 else lon)
                at = 4 * ((r + 1) % 4) + (c + 1) % 4
                send(OUTQ.at[4 * r + c], SKQ.at[at], skip_recv.at[at], to)

    window(0, 0)
    await_halo(0)
    window(0, 1)
    await_halo(1)
    window(1, 0)
    await_halo(2)
    window(1, 1)

    def rows(ref, at):
        return jnp.concatenate([ref[n].astype(F32) for n in at], axis=0).astype(BF16)

    for at in [0, 1, 2, 3, 4, 8, 12]:
        pltpu.make_async_copy(SKQ.at[at], SKQ.at[at], skip_recv.at[at]).wait()
    for r in range(4):
        block = dot(expand[...], rows(SKQ, range(4 * r, 4 * r + 4)))
        SK[:, 3 * r : 3 * r + 3] = block.reshape(2, 3, 24, 512).astype(BF16)
    skip_copy = pltpu.make_async_copy(SK, skip_out, out_sem.at[0])
    skip_copy.start()
    service(4)

    for a, b in [(0, 3), (1, 3), (2, 3), (3, 0), (3, 1), (3, 2), (3, 3)]:
        at = spot(a, b)
        pltpu.make_async_copy(FINE.at[at], FINE.at[at], mid_recv.at[at]).wait()
    joined = []
    for q in range(4):
        parts = dot(merge[...], rows(FINE, range(4 * q, 4 * q + 4)))
        joined.append(jnp.concatenate([parts[p * QUAD : (p + 1) * QUAD] for p in range(4)], axis=1))
    JN[...] = normalized(jnp.concatenate(joined, axis=0))
    bias = score_bias(dot(marks[...], L2[...].reshape(768, 128)).astype(BF16), tile[...])
    service(1)
    while order and order[0][0] < 2:
        service(1)
    await_weights(0)

    def merge_part(n, carry):
        at = pl.ds(pl.multiple_of(n * 256, 256), 256)
        weight = GW[:, 0:64, at].reshape(nlon * 64, 256)
        MG[:, at] = dot(JN[...], weight)
        return carry

    lax.fori_loop(0, 4, merge_part, 0)
    merged = MG[...].astype(BF16).astype(F32)
    JN[:, 0:1024] = normalized(merged)
    while order:
        service(1)
    await_weights(1)
    await_weights(2)

    def qkv_part(n, carry):
        row = pl.ds(pl.multiple_of(64 + 32 * (n // 4), 32), 32)
        at = pl.ds(pl.multiple_of(lax.rem(n, 4) * 256, 256), 256)
        weight = GW[:, row, at].reshape(nlon * 32, 256)
        PK2[n] = dot(JN[:, 0:1024], weight).astype(BF16)
        return carry

    lax.fori_loop(0, 12, qkv_part, 0)

    def heads_part(g, carry):
        MX2[g] = attend(PK2[g], PK2[4 + g], PK2[8 + g], bias).astype(BF16)
        return carry

    lax.fori_loop(0, 4, heads_part, 0)
    mixed = jnp.concatenate([MX2[g] for g in range(4)], axis=1)
    JN[:, 1024:2048] = mixed

    def out_part(n, carry):
        at = pl.ds(pl.multiple_of(n * 256, 256), 256)
        weight = GW[:, 160:192, at].reshape(nlon * 32, 256)
        result = MG[:, at].astype(BF16).astype(F32) + dot(JN[:, 1024:2048], weight)
        for q in range(4):
            COQ[q, :, at] = result[q * QUAD : (q + 1) * QUAD].astype(BF16)
        return carry

    lax.fori_loop(0, 4, out_part, 0)

    CQ[3] = COQ[0]
    send(COQ.at[1], CQ.at[2], back_recv.at[2], (lat, right))
    send(COQ.at[2], CQ.at[1], back_recv.at[1], (down, lon))
    send(COQ.at[3], CQ.at[0], back_recv.at[0], (down, right))
    for at in range(3):
        pltpu.make_async_copy(CQ.at[at], CQ.at[at], back_recv.at[at]).wait()
    for r in range(2):
        block = dot(expand2[...], rows(CQ, (2 * r, 2 * r + 1))).reshape(2, 3, 16, 1024)
        CO[:, 3 * r : 3 * r + 3] = block[:, :, 0:12].astype(BF16)
    coarse_copy = pltpu.make_async_copy(CO, coarse_out, out_sem.at[1])
    coarse_copy.start()
    skip_copy.wait()
    coarse_copy.wait()
    for copy in sends:
        copy.wait_send()
    for c in range(3):
        ref = GW.at[0 : nlon - 1, 0:64]
        pltpu.make_async_copy(ref, ref, drain_sem.at[c]).wait()


def edge_labels(ids):
    height = ids.shape[1]
    global_rows = lax.axis_index("lat") * height + jnp.arange(height)
    edge = (global_rows < 3).astype(jnp.int32)
    return ids * 2 + edge[None, :, None] + 1


def per_device(
    sizes,
    tokens, level_ids, coarse_ids, first_qkv, first_out, merge_weight, second_qkv, second_out,
):
    nlat, nlon = sizes
    spread = lambda a: jnp.broadcast_to(a.astype(BF16)[..., None], a.shape + (128,))
    lab1 = spread(edge_labels(level_ids))
    lab2 = spread(jnp.pad(edge_labels(coarse_ids), ((0, 0), (0, 0), (0, 4))))
    tables = [jnp.asarray(t) for t in one_hot_tables()]
    anywhere = pl.BlockSpec(memory_space=pl.ANY)
    vmem = pl.BlockSpec(memory_space=pltpu.VMEM)
    scratch = [
        pltpu.VMEM((2, 15, 32, 512), BF16),
        pltpu.VMEM((2, 15, 32, 128), BF16),
        pltpu.VMEM((4, 2, 6, 16, 128), BF16),
        pltpu.VMEM((512, 1536), BF16),
        pltpu.VMEM((512, 512), BF16),
        pltpu.VMEM((nlon, 192, 1024), BF16),
        pltpu.VMEM((TOKENS, 1536), BF16),
        pltpu.VMEM((TOKENS, 512), BF16),
        pltpu.VMEM((16, QUAD, 512), BF16),
        pltpu.VMEM((16, QUAD, 512), BF16),
        pltpu.VMEM((16, QUAD, 512), BF16),
        pltpu.VMEM((2, 12, 24, 512), BF16),
        pltpu.VMEM((TOKENS, 1024), F32),
        pltpu.VMEM((TOKENS, 2048), BF16),
        pltpu.VMEM((12, TOKENS, 256), BF16),
        pltpu.VMEM((4, TOKENS, 256), BF16),
        pltpu.VMEM((4, QUAD, 1024), BF16),
        pltpu.VMEM((4, QUAD, 1024), BF16),
        pltpu.VMEM((2, 6, 12, 1024), BF16),
        pltpu.SemaphoreType.DMA((10,)),
        pltpu.SemaphoreType.DMA((9,)),
        pltpu.SemaphoreType.DMA((16,)),
        pltpu.SemaphoreType.DMA((16,)),
        pltpu.SemaphoreType.DMA((3,)),
        pltpu.SemaphoreType.DMA((26,)),
        pltpu.SemaphoreType.DMA((3, nlon)),
        pltpu.SemaphoreType.DMA((3,)),
        pltpu.SemaphoreType.DMA((3,)),
        pltpu.SemaphoreType.DMA((2,)),
    ]
    return pl.pallas_call(
        functools.partial(kernel, sizes),
        out_shape=(
            jax.ShapeDtypeStruct(tokens.shape, BF16),
            jax.ShapeDtypeStruct(coarse_ids.shape + (1024,), BF16),
        ),
        in_specs=[anywhere] * 8 + [vmem] * 6,
        out_specs=(anywhere, anywhere),
        scratch_shapes=scratch,
        compiler_params=pltpu.CompilerParams(
            collective_id=0, has_side_effects=True, vmem_limit_bytes=56 * 1024 * 1024
        ),
        name="swin",
    )(
        tokens, lab1, lab2, first_qkv, first_out, merge_weight, second_qkv, second_out, *tables
    )


def solution(mesh):
    placed = (
        P(None, "lat", "lon", None),
        P(None, "lat", "lon"),
        P(None, "lat", "lon"),
        P(),
        P(),
        P("lon", None),
        P("lon", None),
        P("lon", None),
    )
    return jax.shard_map(
        functools.partial(per_device, (mesh.shape["lat"], mesh.shape["lon"])),
        mesh=mesh,
        in_specs=placed,
        out_specs=(P(None, "lat", "lon", None), P(None, "lat", "lon", None)),
        check_vma=False,
    )
```

time: 258 us -> 111 us (0.43); the launches traced: 254 us -> 110 us
  waiting for transfers between devices: 110 us -> 0 us
  Pallas kernels: 0 us -> 103 us
  starting transfers between devices: 64.1 us -> 0 us
  matrix products: 31 us -> 0 us
  local copies, waits for them, and re-layouts: 28.2 us -> 5.47 us
  between operations: 14.3 us -> 0.67 us
  other arithmetic: 6.58 us -> 1.57 us
    pallas_call x0 -> x1, Pallas kernels: none -> 103 us  [per_device(): pl.pallas_call(functools.partial(kernel, sizes), out_shape=(jax.ShapeDtyp...]
    all_gather x3 -> x0, waiting for transfers between devices: 90.2 us -> none  [the longest x1 49 us: second_out_product(): return add_rows(left, lax.all_gather(second_out, 'lon', axis=0, tiled=True))]
    ppermute x12 -> x0, starting transfers between devices: 64 us -> none  [from_behind(): return lax.ppermute(block, axis, route)]
    dot_general x8 -> x0, matrix products: 20.2 us -> none  [the longest x3 10.1 us: add_rows(): return jnp.dot(left, piece, preferred_element_type=jnp.float32)]
    ppermute x12 -> x0, waiting for transfers between devices: 18 us -> none  [from_behind(): return lax.ppermute(block, axis, route)]
    sub x3 -> x0, matrix products: 10.7 us -> none  [window_softmax(): expos = jnp.exp(scores - highest)]
    convert_element_type x9 -> x1, local copies, waits for them, and re-layouts: 7.85 us -> 0.01 us  [per_device(): a.astype(BF16)[..., None]]
    slice x10 -> x0, local copies, waits for them, and re-layouts: 4.1 us -> none  [the longest x2 1.08 us: shifted_layer(): moved = jnp.concatenate([field[:, half_rows:], below[0]], axis=1)]
  transfers between devices with their start and end apart: 15 -> 0, of which waited for: 10 -> 0; matrix products, arithmetic and copies ran while one was open for 24% -> 0% of each run, Pallas kernels for 0% -> 0%
where the time goes in v1:
time: 111 us; the launch traced here: 110 us
  Pallas kernels  103 us (93%)
  local copies, waits for them, and re-layouts  5.47 us (5%)
  other arithmetic  1.57 us (1%)
    pallas_call x1, Pallas kernels, per_device(): pl.pallas_call(functools.partial(kernel, sizes), out_shape=(jax.ShapeDtyp...  103 us

profile of v1, /device:TPU:1, one launch (start us, length us, event | category | flops | bytes accessed | tf_op | source)
XLA Modules:
  0.0 110.5 jit_solution(16109707027744848003)
XLA Ops:
  0.7 0.8 add_convert_fusion.1
  1.4 0.8 add_convert_fusion
  2.3 0.7 broadcast_in_dim.5.lab2
  3.0 0.8 broadcast_in_dim.4.lab1
  3.8 102.8 %swin.1 = (bf16[2,12,24,512]{3,2,1,0:T(8,128)(2,1)}, bf16[2,6,12,1024]{3,2,1,0:T(8,128)(2,1)}) custom-call(bf16[2,12,24,512]{3,2,1,0:T(8,128)(2,1)} %tokens.1, bf16[2,12,24,128]{3,2,1,0:T(8,128)(2,1)} %broadcast_in_dim.4.lab1, bf16[2,6,16,128]{3,2,1,0:T(8,128)(2,1)} %broadcast_in_dim.5.lab2, bf16[512,1536]{1,0:T(8,128)(2,1)} %first_qkv.1, ...), custom_call_target="tpu_custom_call" | custom-call | tf_op jit(solution)/shard_map/swin/pallas_call | solution.py:430
  106.5 2.0 %copy.18 = bf16[2,6,12,1024]{3,0,2,1:T(2,128)(2,1)} copy(bf16[2,6,12,1024]{3,2,1,0:T(8,128)(2,1)} %get-tuple-element.3) | data formatting | bytes 589824 | tf_op jit(solution)/shard_map/swin/pallas_call | solution.py:430
  108.5 1.9 %copy.21 = bf16[2,12,24,512]{3,2,1,0:T(8,128)(2,1)} copy(bf16[2,12,24,512]{3,2,1,0:T(8,128)(2,1)} %get-tuple-element.6) | data formatting | bytes 1179648
  (5 shorter events, 0.0 us)
